TPU v7x, 256 devices: a whole 4x4x8 slice. The times are simulated.
256 devices in a mesh: expert: 32 (over x, z), vocab: 8 (over y, core).
Axes of the slice: x: 4, y: 4, z: 8, core: 2. Of those that a mesh axis runs over, the one named last changes fastest.
Arguments:
- out_grad: bfloat16 [4096, 4096], P('expert', 'vocab'), may hold values from -6 to 6
- residual_stream: bfloat16 [4096, 4096], P('expert', 'vocab'), may hold values from -228 to 228
- norm_gain: float32 [4096], P('vocab'), may hold values from 0.25 to 51
- expert_ids: int32 [4096, 8], P('expert'), may hold values from 0 to 31, all different within a row; in each aligned block of 128 rows (0 to 127, 128 to 255, ...) at most 38 rows name the same one
- gate_scores: float32 [4096, 8], P('expert'), may hold values from 0.05 to 1
- saved_gate: bfloat16 [32, 1216, 1536], P('expert', None, 'vocab'), may hold values from -6 to 6
- saved_up: bfloat16 [32, 1216, 1536], P('expert', None, 'vocab'), may hold values from -6 to 6
- gate_weight: bfloat16 [32, 4096, 1536], P('expert', None, 'vocab'), may hold values from -0.09375 to 0.09375
- up_weight: bfloat16 [32, 4096, 1536], P('expert', None, 'vocab'), may hold values from -0.09375 to 0.09375
- down_weight: bfloat16 [32, 1536, 4096], P('expert', 'vocab'), may hold values from -0.15625 to 0.15625
- embedding: bfloat16 [98304, 4096], P(('expert', 'vocab')), may hold values from -0.09375 to 0.09375
- allowed: int32 [98304], P(('expert', 'vocab')), may hold values 0 or 1
- suffix_start: int32 [32], P('expert'), may hold values from 0 to 108
Outputs:
- token_grad: bfloat16 [4096, 4096], P('expert', 'vocab')
- scores: float32 [640, 98304], P(None, ('expert', 'vocab'))
Inputs may be any that keep to these rules, and one draw needn't show every extreme that they name: `expert_ids`: in each aligned block of 128 rows (one behavior) a row names 8 different experts and no expert is named by more than 38 rows; some expert is named by exactly 38 rows in some blocks.
All inputs are finite; a program needn't handle non-finite values. No bound on the sum of `allowed` on one device may be relied on, other than what follows from the above.
Results may differ from a plain program's by a relative error of at most 0.01.
Values may be sent and summed in bfloat16 or wider, within the bound.
No kernel may reach another device: no remote copies, remote signals or barrier semaphores. Data moves between devices by JAX's collectives and lax.ppermute only.
A program may use at most 128 MiB of HBM per device.

v0:
```python
import jax
import jax.numpy as jnp
from jax import lax
from jax.sharding import PartitionSpec as P

D = 4096
SUFFIX = 20


def sent_to_all(value, axis):
    peers = lax.axis_size(axis)
    return lax.all_to_all(
        jnp.broadcast_to(value[None], (peers, *value.shape)), axis, 0, 0, tiled=True
    )


def taken_together(value, axis):
    everything = sent_to_all(value, axis)
    return jnp.sum(everything, axis=0)


def in_order(parts, dim):
    parts = jnp.moveaxis(parts, 0, dim)
    lengths = parts.shape
    return parts.reshape(*lengths[:dim], lengths[dim] * lengths[dim + 1], *lengths[dim + 2 :])


def collect(value, axis, dim):
    return in_order(sent_to_all(value, axis), dim)


def shards(
    out_grad,
    residual_stream,
    norm_gain,
    expert_ids,
    gate_scores,
    saved_gate,
    saved_up,
    gate_weight,
    up_weight,
    down_weight,
    embedding,
    allowed,
    suffix_start,
):
    n_expert = lax.axis_size("expert")
    seq_len, d_slice = out_grad.shape
    top_k = expert_ids.shape[1]
    slot_count = saved_gate.shape[1]
    capacity = slot_count // n_expert
    contract = (((1,), (1,)), ((), ()))
    chosen = expert_ids.reshape(-1)
    matches = (chosen[:, None] == jnp.arange(n_expert, dtype=jnp.int32)[None, :]).astype(jnp.int32)
    before = jnp.cumsum(matches, axis=0) - matches
    position = jnp.sum(before * matches, axis=1)
    target = chosen * capacity + position
    gate_share = gate_scores / jnp.sum(gate_scores, axis=1, keepdims=True)
    routed = (gate_share[:, :, None] * out_grad.astype(jnp.float32)[:, None, :]).astype(
        jnp.bfloat16
    )
    routed = routed.reshape(seq_len * top_k, d_slice)
    buffer = jnp.zeros((slot_count, d_slice), jnp.bfloat16).at[target].set(routed)
    arrived = lax.all_to_all(buffer, "expert", split_axis=0, concat_axis=0, tiled=True)
    incoming = lax.all_gather(arrived, "vocab", axis=1, tiled=True)
    act_grad = lax.dot_general(
        incoming, down_weight[0], contract, preferred_element_type=jnp.float32
    )
    pre_gate = saved_gate[0].astype(jnp.float32)
    pre_up = saved_up[0].astype(jnp.float32)
    sigmoid_g = jax.nn.sigmoid(pre_gate)
    gate_grad = (act_grad * pre_up * sigmoid_g * (1.0 + pre_gate * (1.0 - sigmoid_g))).astype(
        jnp.bfloat16
    )
    up_grad = (act_grad * pre_gate * sigmoid_g).astype(jnp.bfloat16)
    partial_value = lax.dot_general(
        gate_grad, gate_weight[0], contract, preferred_element_type=jnp.float32
    )
    partial_value = partial_value + lax.dot_general(
        up_grad, up_weight[0], contract, preferred_element_type=jnp.float32
    )
    partial_rounded = partial_value.astype(jnp.bfloat16)
    slot_grad = lax.psum_scatter(partial_rounded, "vocab", scatter_dimension=1, tiled=True).astype(
        jnp.float32
    )
    returned = lax.all_to_all(
        slot_grad.astype(jnp.bfloat16), "expert", split_axis=0, concat_axis=0, tiled=True
    ).astype(slot_grad.dtype)
    moe_grad = jnp.sum(returned[target].reshape(seq_len, top_k, d_slice), axis=1)
    resid = residual_stream.astype(jnp.float32)
    sum_squares = taken_together(jnp.sum(resid * resid, axis=1), "vocab")
    inverse = lax.rsqrt(sum_squares / D + 1e-06)
    normed = resid * inverse[:, None]
    scaled = moe_grad * norm_gain[None, :]
    row_project = taken_together(jnp.sum(scaled * normed, axis=1), "vocab") / D
    token_grad = (
        out_grad.astype(jnp.float32) + inverse[:, None] * (scaled - normed * row_project[:, None])
    ).astype(jnp.bfloat16)
    suffix_grad = lax.dynamic_slice_in_dim(token_grad, suffix_start[0], SUFFIX, 0)
    suffix_grad = collect(suffix_grad, "vocab", 1)
    raw_scores = -lax.dot_general(
        lax.all_gather(suffix_grad, "expert", axis=0, tiled=True),
        embedding,
        contract,
        preferred_element_type=jnp.float32,
    )
    scores = jnp.where(allowed[None, :] > 0, raw_scores, jnp.float32(0.0))
    return (token_grad, scores)


def solution(mesh):
    placed = (
        P("expert", "vocab"),
        P("expert", "vocab"),
        P("vocab"),
        P("expert", None),
        P("expert", None),
        P("expert", None, "vocab"),
        P("expert", None, "vocab"),
        P("expert", None, "vocab"),
        P("expert", None, "vocab"),
        P("expert", "vocab", None),
        P(("expert", "vocab"), None),
        P(("expert", "vocab")),
        P("expert"),
    )
    return jax.shard_map(
        shards,
        mesh=mesh,
        in_specs=placed,
        out_specs=(P("expert", "vocab"), P(None, ("expert", "vocab"))),
        check_vma=False,
    )
```

profile of v0, /device:TPU:8, one launch (start us, length us, event | category | flops | bytes accessed | tf_op | source)
XLA Modules:
  0.0 413.3 jit_solution(6126934621142170420)
XLA Ops:
  7.2 0.9 copy.37
  9.1 9.0 %reduce-window.6 = s32[32,8,128]{2,1,0:T(8,128)S(1)} reduce-window(s32[32,8,128]{2,1,0:T(8,128)S(1)} %fusion.39, s32[]{:T(128)} %constant.7.clone.1), window={size=1x1x128 pad=0_0x0_0x127_0}, to_apply=%region_2.3 | reduce-window | flops 4161536 | bytes 262148 | tf_op jit(solution)/shard_map/reduce-window
  18.7 0.9 convert_element_type.50
  19.7 0.7 reduce_sum.69
  21.0 0.7 copy.41
  21.8 0.9 mul.97
  22.8 6.6 %scatter_custom_fusion = bf16[1216,512]{1,0:T(8,128)(2,1)} fusion(s32[1024]{0:T(1024)S(1)} %bitcast.66, f32[128,512]{1,0:T(8,128)S(1)} %convert_element_type.50, f32[1024]{0:T(1024)S(1)} %mul.97, bf16[]{:T(256)} %constant.5.clone.1), kind=kCustom, calls=%fused_computation.16 | custom fusion | flops 1048576 | bytes 1511426 | tf_op jit(solution)/shard_map/scatter | solution.py:63
  29.4 2.3 all_to_all.26
  31.7 46.4 %all_to_all.38 = bf16[32,38,512]{2,1,0:T(8,128)(2,1)} all-to-all(bf16[32,38,512]{2,1,0:T(8,128)(2,1)} %all_to_all.26), channel_id=1, replica_groups=mesh['expert'=32,'vocab'=8] {'expert'}, dimensions={0} | all-to-all | bytes 2490368 | tf_op jit(solution)/shard_map/all_to_all | solution.py:64
  78.1 2.3 all_to_all.28
  80.4 54.2 %all-gather.4.cloned.1.call-done = bf16[1216,4096]{1,0:T(8,128)(2,1)} async-done(((bf16[1216,512]{1,0:T(8,128)(2,1)}), bf16[1216,4096]{1,0:T(8,128)(2,1)}) %all-gather.4.cloned.1.call-update) | async-done | bytes 9961488 | tf_op jit(solution)/shard_map/all_gather | solution.py:65
  134.6 7.6 %fusion.4 = f32[1216,192]{0,1:T(8,128)S(1)} fusion(bf16[1216,4096]{1,0:T(8,128)(2,1)} %all-gather.4.cloned.1.call-done, bf16[1,192,4096]{2,1,0:T(8,128)(2,1)} %param.22), kind=kOutput, calls=%fused_computation.9 | convolution fusion | flops 1912602624 | bytes 12468224 | tf_op jit(solution)/shard_map/dot_general | solution.py:66
  142.2 0.9 copy-done.1
  143.2 8.4 %fusion.2 = f32[1216,4096]{1,0:T(8,128)} fusion(bf16[1,4096,192]{1,2,0:T(8,128)(2,1)S(1)} %copy-done.3, f32[1216,192]{0,1:T(8,128)S(1)} %fusion.4, bf16[1,1216,192]{1,2,0:T(8,128)(2,1)S(1)} %copy-done.5, bf16[1,1216,192]{1,2,0:T(8,128)(2,1)S(1)} %copy-done.2), kind=kOutput, calls=%fused_computation.7 | convolution fusion | flops 1915404288 | bytes 23363584 | tf_op jit(solution)/shard_map/dot_general | solution.py:76
  151.6 14.2 %add_convert_fusion = bf16[1216,4096]{1,0:T(8,128)(2,1)} fusion(f32[1216,4096]{1,0:T(8,128)} %fusion.2, bf16[1,4096,192]{1,2,0:T(8,128)(2,1)} %param.21, f32[1216,192]{0,1:T(8,128)} %copy-done.1, bf16[1,1216,192]{1,2,0:T(8,128)(2,1)} %param.18), kind=kOutput, calls=%fused_computation.2 | convolution fusion | flops 1924198400 | bytes 32858112 | tf_op jit(solution)/shard_map/dot_general | solution.py:79
  165.7 0.9 copy-done.4
  167.3 4.5 %all-to-all-start = ((f32[8,1,128]{2,1,0:T(1,128)}), f32[8,1,128]{2,1,0:T(1,128)S(1)}, u32[]{:S(2)}, u32[]{:S(2)}) async-start(f32[8,1,128]{2,1,0:T(1,128)} %broadcast_in_dim.16), calls=%async_computation | async-start | bytes 8192 | tf_op jit(solution)/shard_map/all_to_all | solution.py:12
  171.9 55.1 %reduce-scatter.2.cloned.1.call-done = bf16[1216,512]{1,0:T(8,128)(2,1)} async-done(((bf16[1216,4096]{1,0:T(8,128)(2,1)}), bf16[1216,512]{1,0:T(8,128)(2,1)}) %reduce-scatter.2.cloned.1.call-update) | async-done | bytes 1245200 | tf_op jit(solution)/shard_map/reduce_scatter | solution.py:83
  227.0 2.3 all_to_all.29
  229.3 10.2 %all-to-all-start.2 = ((bf16[32,38,512]{2,1,0:T(8,128)(2,1)}), bf16[32,38,512]{2,1,0:T(8,128)(2,1)}, u32[]{:S(2)}, u32[]{:S(2)}) async-start(bf16[32,38,512]{2,1,0:T(8,128)(2,1)} %all_to_all.29), calls=%async_computation.3 | async-start | bytes 2621440 | tf_op jit(solution)/shard_map/all_to_all | solution.py:86
  239.5 34.5 %all-to-all-done.2 = bf16[32,38,512]{2,1,0:T(8,128)(2,1)} async-done(((bf16[32,38,512]{2,1,0:T(8,128)(2,1)}), bf16[32,38,512]{2,1,0:T(8,128)(2,1)}, u32[]{:S(2)}, u32[]{:S(2)}) %all-to-all-start.2) | async-done | bytes 1245216 | tf_op jit(solution)/shard_map/all_to_all | solution.py:86
  274.0 2.7 reshape.102
  276.7 7.0 %gather_fusion = f32[1024,512]{1,0:T(8,128)} fusion(f32[1216,512]{1,0:T(8,128)} %reshape.102, s32[1024]{0:T(1024)S(1)} %broadcast_clamp_fusion), kind=kCustom, calls=%fused_computation | custom fusion | bytes 4198400 | tf_op jit(solution)/shard_map/gather | solution.py:89
  283.6 2.1 bitcast_reduce_fusion
  286.6 5.1 %all-to-all-start.3 = ((f32[8,1,128]{2,1,0:T(1,128)}), f32[8,1,128]{2,1,0:T(1,128)S(1)}, u32[]{:S(2)}, u32[]{:S(2)}) async-start(f32[8,1,128]{2,1,0:T(1,128)} %broadcast_in_dim.18), calls=%async_computation.4 | async-start | bytes 8192 | tf_op jit(solution)/shard_map/all_to_all | solution.py:12
  292.4 3.1 all-to-all-done.3
  296.6 1.1 fusion.34
  297.8 9.2 %all_to_all.39 = bf16[8,20,512]{2,1,0:T(8,128)(2,1)S(1)} all-to-all(bf16[8,20,512]{2,1,0:T(8,128)(2,1)S(1)} %broadcast_in_dim.20), channel_id=1, replica_groups=mesh['expert'=32,'vocab'=8] {'vocab'}, dimensions={0} | all-to-all | bytes 327680 | tf_op jit(solution)/shard_map/all_to_all | solution.py:12
  307.0 0.8 reshape.119
  307.9 84.7 %all-gather.6.cloned.1.call-done = bf16[32,20,4096]{2,1,0:T(8,128)(2,1)} async-done(((bf16[1,20,4096]{2,1,0:T(8,128)(2,1)}), bf16[32,20,4096]{2,1,0:T(8,128)(2,1)}) %all-gather.6.cloned.1.call-update) | async-done | bytes 5242896 | tf_op jit(solution)/shard_map/all_gather | solution.py:102
  392.6 7.8 %reshape.120 = bf16[640,4096]{1,0:T(8,128)(2,1)} reshape(bf16[32,20,4096]{2,1,0:T(8,128)(2,1)} %all-gather.6.cloned.1.call-done) | data formatting | bytes 10485760
  400.4 6.3 %fusion.6 = f32[640,384]{1,0:T(8,128)} fusion(bf16[640,4096]{1,0:T(8,128)(2,1)} %reshape.120, bf16[384,4096]{1,0:T(8,128)(2,1)S(1)} %copy-done, pred[384]{0:T(512)(128)(4,1)S(1)} %broadcast_compare_fusion), kind=kOutput, calls=%fused_computation.15 | convolution fusion | flops 2013757440 | bytes 9372032 | tf_op jit(solution)/shard_map/dot_general | solution.py:101
  (51 shorter events, 5.2 us)
Async XLA Ops:
  7.2 393.3 %copy-start = (bf16[384,4096]{1,0:T(8,128)(2,1)S(1)}, bf16[384,4096]{1,0:T(8,128)(2,1)}, u32[]{:S(2)}) copy-start(bf16[384,4096]{1,0:T(8,128)(2,1)} %param.23) | copy-start | bytes 9437188
  7.2 127.4 %all-gather.4.cloned.1.call-start = ((), (), s32[]{:S(2)}) async-start(), calls=%async_computation.6 | async-start | bytes 11206656 | tf_op jit(solution)/shard_map/all_gather | solution.py:65
  80.4 146.6 %reduce-scatter.2.cloned.1.call-start = ((), (), s32[]{:S(2)}) async-start(), calls=%async_computation.7 | async-start | bytes 11206656 | tf_op jit(solution)/shard_map/reduce_scatter | solution.py:83
  134.6 8.6 %copy-start.2 = (bf16[1,1216,192]{1,2,0:T(8,128)(2,1)S(1)}, bf16[1,1216,192]{1,2,0:T(8,128)(2,1)}, u32[]{:S(2)}) copy-start(bf16[1,1216,192]{1,2,0:T(8,128)(2,1)} %param.18) | copy-start | bytes 1400836
  134.6 8.6 %copy-start.3 = (bf16[1,4096,192]{1,2,0:T(8,128)(2,1)S(1)}, bf16[1,4096,192]{1,2,0:T(8,128)(2,1)}, u32[]{:S(2)}) copy-start(bf16[1,4096,192]{1,2,0:T(8,128)(2,1)} %param.20) | copy-start | bytes 4718596
  134.6 8.6 %copy-start.5 = (bf16[1,1216,192]{1,2,0:T(8,128)(2,1)S(1)}, bf16[1,1216,192]{1,2,0:T(8,128)(2,1)}, u32[]{:S(2)}) copy-start(bf16[1,1216,192]{1,2,0:T(8,128)(2,1)} %param.19) | copy-start | bytes 1400836
  142.2 0.9 copy-start.1
  165.7 0.9 copy-start.4
  167.3 62.0 %all-to-all-start = ((f32[8,1,128]{2,1,0:T(1,128)}), f32[8,1,128]{2,1,0:T(1,128)S(1)}, u32[]{:S(2)}, u32[]{:S(2)}) async-start(f32[8,1,128]{2,1,0:T(1,128)} %broadcast_in_dim.16), calls=%async_computation | async-start | bytes 8192 | tf_op jit(solution)/shard_map/all_to_all | solution.py:12
  229.3 44.7 %all-to-all-start.2 = ((bf16[32,38,512]{2,1,0:T(8,128)(2,1)}), bf16[32,38,512]{2,1,0:T(8,128)(2,1)}, u32[]{:S(2)}, u32[]{:S(2)}) async-start(bf16[32,38,512]{2,1,0:T(8,128)(2,1)} %all_to_all.29), calls=%async_computation.3 | async-start | bytes 2621440 | tf_op jit(solution)/shard_map/all_to_all | solution.py:86
  283.6 2.1 copy-start.7
  283.6 24.2 %copy-start.8 = (s32[384]{0:T(512)S(1)}, s32[384]{0:T(512)}, u32[]{:S(2)}) copy-start(s32[384]{0:T(512)} %param.24) | copy-start | bytes 4612
  286.6 8.9 %all-to-all-start.3 = ((f32[8,1,128]{2,1,0:T(1,128)}), f32[8,1,128]{2,1,0:T(1,128)S(1)}, u32[]{:S(2)}, u32[]{:S(2)}) async-start(f32[8,1,128]{2,1,0:T(1,128)} %broadcast_in_dim.18), calls=%async_computation.4 | async-start | bytes 8192 | tf_op jit(solution)/shard_map/all_to_all | solution.py:12
  291.7 100.9 %all-gather.6.cloned.1.call-start = ((), (), s32[]{:S(2)}) async-start(), calls=%async_computation.8 | async-start | bytes 6488064 | tf_op jit(solution)/shard_map/all_gather | solution.py:102
  297.7 9.3 %copy-start.6 = (bf16[128,512]{1,0:T(8,128)(2,1)}, bf16[128,512]{1,0:T(8,128)(2,1)S(1)}, u32[]{:S(2)}) copy-start(bf16[128,512]{1,0:T(8,128)(2,1)S(1)} %fusion.34) | copy-start | bytes 393220
Sparse Core Ops, SparseCore 0:
  80.5 54.0 all-gather.3
  165.9 61.0 reduce-scatter.1
  308.0 84.5 all-gather.5
where the time goes:
time: 414 us; the launch traced here: 413 us
  waiting for transfers between devices  232 us (56%)
  blocking collectives  55.6 us (13%)
  matrix products  36.5 us (9%)
  local copies, waits for them, and re-layouts  31.6 us (8%)
  other arithmetic  23.5 us (6%)
  starting transfers between devices  19.9 us (5%)
  between operations  14.6 us (4%)
    all_gather x1, waiting for transfers between devices, shards(): lax.all_gather(suffix_grad, 'expert', axis=0, tiled=True)  84.7 us
    reduce_scatter x1, waiting for transfers between devices, shards(): lax.psum_scatter(partial_rounded, 'vocab', scatter_dimension=1, tiled=True)  55.1 us
    all_gather x1, waiting for transfers between devices, shards(): incoming = lax.all_gather(arrived, 'vocab', axis=1, tiled=True)  54.2 us
    all_to_all x1, blocking collectives, shards(): lax.all_to_all(buffer, 'expert', split_axis=0, concat_axis=0, tiled=True)  46.4 us
    all_to_all x1, waiting for transfers between devices, shards(): lax.all_to_all(slot_grad.astype(jnp.bfloat16), 'expert', split_axis=0, co...  34.5 us
    dot_general x1, matrix products, shards(): lax.dot_general(up_grad, up_weight[0], contract, preferred_element_type=j...  14.2 us
    unnamed x21, local copies, waits for them, and re-layouts  11.4 us
    all_to_all x1, starting transfers between devices, shards(): lax.all_to_all(slot_grad.astype(jnp.bfloat16), 'expert', split_axis=0, co...  10.2 us
  transfers between devices with their start and end apart: 6, of which 5 were waited for; matrix products, arithmetic and copies ran while one was open for 0% of the time, Pallas kernels for 0%

commit v1 on v0

--- a/solution.py
+++ b/solution.py
@@ -99,7 +99,10 @@
     suffix_grad = lax.dynamic_slice_in_dim(token_grad, suffix_start[0], SUFFIX, 0)
     suffix_grad = collect(suffix_grad, "vocab", 1)
     raw_scores = -lax.dot_general(
-        lax.all_gather(suffix_grad, "expert", axis=0, tiled=True),
+        jnp.concatenate(
+            lax.all_to_all(jnp.stack([suffix_grad] * lax.axis_size("expert")), "expert", 0, 0),
+            axis=0,
+        ),
         embedding,
         contract,
         preferred_element_type=jnp.float32,

time: 414 us -> 479 us (1.16)
  waiting for transfers between devices: 232 us -> 288 us
  starting transfers between devices: 19.9 us -> 26 us
    all_to_all x0 -> x1, waiting for transfers between devices: none -> 141 us  [shards(): lax.all_to_all(jnp.stack([suffix_grad] * lax.axis_size('expert')), 'exper...]
    all_gather x1 -> x0, waiting for transfers between devices: 84.7 us -> none  [shards(): lax.all_gather(suffix_grad, 'expert', axis=0, tiled=True)]
    unnamed x21, local copies, waits for them, and re-layouts: 11.4 us -> 2.87 us
    reshape x0 -> x1, local copies, waits for them, and re-layouts: none -> 7.84 us  [shards(): jnp.concatenate(lax.all_to_all(jnp.stack([suffix_grad] * lax.axis_size('e...]
    all_to_all x0 -> x1, starting transfers between devices: none -> 6.05 us  [shards(): lax.all_to_all(jnp.stack([suffix_grad] * lax.axis_size('expert')), 'exper...]
where the time goes in v1:
time: 479 us; the launch traced here: 477 us
  waiting for transfers between devices  288 us (60%)
  blocking collectives  55.6 us (12%)
  matrix products  36.5 us (8%)
  local copies, waits for them, and re-layouts  34.3 us (7%)
  starting transfers between devices  26 us (5%)
  other arithmetic  22.3 us (5%)
  between operations  14.9 us (3%)
    all_to_all x1, waiting for transfers between devices, shards(): lax.all_to_all(jnp.stack([suffix_grad] * lax.axis_size('expert')), 'exper...  141 us
    reduce_scatter x1, waiting for transfers between devices, shards(): lax.psum_scatter(partial_rounded, 'vocab', scatter_dimension=1, tiled=True)  55.1 us
    all_gather x1, waiting for transfers between devices, shards(): incoming = lax.all_gather(arrived, 'vocab', axis=1, tiled=True)  54.2 us
    all_to_all x1, blocking collectives, shards(): lax.all_to_all(buffer, 'expert', split_axis=0, concat_axis=0, tiled=True)  46.4 us
    all_to_all x1, waiting for transfers between devices, shards(): lax.all_to_all(slot_grad.astype(jnp.bfloat16), 'expert', split_axis=0, co...  34.5 us
    dot_general x1, matrix products, shards(): lax.dot_general(up_grad, up_weight[0], contract, preferred_element_type=j...  14.2 us
    all_to_all x1, starting transfers between devices, shards(): lax.all_to_all(slot_grad.astype(jnp.bfloat16), 'expert', split_axis=0, co...  10.2 us
    all_to_all x2, starting transfers between devices, sent_to_all(): lax.all_to_all(jnp.broadcast_to(value[None], (peers, *value.shape)), axis...  9.67 us
  transfers between devices with their start and end apart: 6, of which 5 were waited for; matrix products, arithmetic and copies ran while one was open for 0% of the time, Pallas kernels for 0%

profile of v1, /device:TPU:8, one launch (start us, length us, event | category | flops | bytes accessed | tf_op | source)
XLA Modules:
  0.0 477.1 jit_solution(7408411396727869910)
XLA Ops:
  7.2 0.9 copy.37
  9.1 9.0 %reduce-window.6 = s32[32,8,128]{2,1,0:T(8,128)S(1)} reduce-window(s32[32,8,128]{2,1,0:T(8,128)S(1)} %fusion.39, s32[]{:T(128)} %constant.7.clone.1), window={size=1x1x128 pad=0_0x0_0x127_0}, to_apply=%region_2.3 | reduce-window | flops 4161536 | bytes 262148 | tf_op jit(solution)/shard_map/reduce-window
  18.7 0.9 convert_element_type.50
  21.0 0.7 copy.41
  21.8 0.9 mul.97
  22.8 6.6 %scatter_custom_fusion = bf16[1216,512]{1,0:T(8,128)(2,1)} fusion(s32[1024]{0:T(1024)S(1)} %bitcast.71, f32[128,512]{1,0:T(8,128)S(1)} %convert_element_type.50, f32[1024]{0:T(1024)S(1)} %mul.97, bf16[]{:T(256)} %constant.5.clone.1), kind=kCustom, calls=%fused_computation.16 | custom fusion | flops 1048576 | bytes 1511426 | tf_op jit(solution)/shard_map/scatter | solution.py:63
  29.4 2.3 all_to_all.29
  31.7 46.4 %all_to_all.43 = bf16[32,38,512]{2,1,0:T(8,128)(2,1)} all-to-all(bf16[32,38,512]{2,1,0:T(8,128)(2,1)} %all_to_all.29), channel_id=1, replica_groups=mesh['expert'=32,'vocab'=8] {'expert'}, dimensions={0} | all-to-all | bytes 2490368 | tf_op jit(solution)/shard_map/all_to_all | solution.py:64
  78.1 2.3 all_to_all.31
  80.4 54.2 %all-gather.2.cloned.1.call-done = bf16[1216,4096]{1,0:T(8,128)(2,1)} async-done(((bf16[1216,512]{1,0:T(8,128)(2,1)}), bf16[1216,4096]{1,0:T(8,128)(2,1)}) %all-gather.2.cloned.1.call-update) | async-done | bytes 9961488 | tf_op jit(solution)/shard_map/all_gather | solution.py:65
  134.6 7.6 %fusion.4 = f32[1216,192]{0,1:T(8,128)S(1)} fusion(bf16[1216,4096]{1,0:T(8,128)(2,1)} %all-gather.2.cloned.1.call-done, bf16[1,192,4096]{2,1,0:T(8,128)(2,1)} %param.22), kind=kOutput, calls=%fused_computation.9 | convolution fusion | flops 1912602624 | bytes 12468224 | tf_op jit(solution)/shard_map/dot_general | solution.py:66
  142.2 0.9 copy-done.1
  143.2 8.4 %fusion.2 = f32[1216,4096]{1,0:T(8,128)} fusion(bf16[1,4096,192]{1,2,0:T(8,128)(2,1)S(1)} %copy-done.3, f32[1216,192]{0,1:T(8,128)S(1)} %fusion.4, bf16[1,1216,192]{1,2,0:T(8,128)(2,1)S(1)} %copy-done.5, bf16[1,1216,192]{1,2,0:T(8,128)(2,1)S(1)} %copy-done.2), kind=kOutput, calls=%fused_computation.7 | convolution fusion | flops 1915404288 | bytes 23363584 | tf_op jit(solution)/shard_map/dot_general | solution.py:76
  151.6 14.2 %add_convert_fusion = bf16[1216,4096]{1,0:T(8,128)(2,1)} fusion(f32[1216,4096]{1,0:T(8,128)} %fusion.2, bf16[1,4096,192]{1,2,0:T(8,128)(2,1)} %param.21, f32[1216,192]{0,1:T(8,128)} %copy-done.1, bf16[1,1216,192]{1,2,0:T(8,128)(2,1)} %param.18), kind=kOutput, calls=%fused_computation.2 | convolution fusion | flops 1924198400 | bytes 32858112 | tf_op jit(solution)/shard_map/dot_general | solution.py:79
  165.7 0.9 copy-done.4
  167.3 4.5 all-to-all-start
  171.9 55.1 %reduce-scatter.2.cloned.1.call-done = bf16[1216,512]{1,0:T(8,128)(2,1)} async-done(((bf16[1216,4096]{1,0:T(8,128)(2,1)}), bf16[1216,512]{1,0:T(8,128)(2,1)}) %reduce-scatter.2.cloned.1.call-update) | async-done | bytes 1245200 | tf_op jit(solution)/shard_map/reduce_scatter | solution.py:83
  227.0 2.3 all_to_all.32
  229.3 10.2 %all-to-all-start.2 = ((bf16[32,38,512]{2,1,0:T(8,128)(2,1)}), bf16[32,38,512]{2,1,0:T(8,128)(2,1)}, u32[]{:S(2)}, u32[]{:S(2)}) async-start(bf16[32,38,512]{2,1,0:T(8,128)(2,1)} %all_to_all.32), calls=%async_computation.3 | async-start | bytes 2621440 | tf_op jit(solution)/shard_map/all_to_all | solution.py:86
  239.5 34.5 %all-to-all-done.2 = bf16[32,38,512]{2,1,0:T(8,128)(2,1)} async-done(((bf16[32,38,512]{2,1,0:T(8,128)(2,1)}), bf16[32,38,512]{2,1,0:T(8,128)(2,1)}, u32[]{:S(2)}, u32[]{:S(2)}) %all-to-all-start.2) | async-done | bytes 1245216 | tf_op jit(solution)/shard_map/all_to_all | solution.py:86
  274.0 2.7 reshape.104
  276.7 7.0 %gather_fusion = f32[1024,512]{1,0:T(8,128)} fusion(f32[1216,512]{1,0:T(8,128)} %reshape.104, s32[1024]{0:T(1024)S(1)} %broadcast_clamp_fusion), kind=kCustom, calls=%fused_computation | custom fusion | bytes 4198400 | tf_op jit(solution)/shard_map/gather | solution.py:89
  283.6 2.1 bitcast_reduce_fusion
  286.5 5.1 %all-to-all-start.3 = ((f32[8,1,128]{2,1,0:T(1,128)}), f32[8,1,128]{2,1,0:T(1,128)S(1)}, u32[]{:S(2)}, u32[]{:S(2)}) async-start(f32[8,1,128]{2,1,0:T(1,128)} %broadcast_in_dim.18), calls=%async_computation.4 | async-start | bytes 8192 | tf_op jit(solution)/shard_map/all_to_all | solution.py:12
  292.3 3.1 all-to-all-done.3
  295.5 1.1 fusion.34
  296.6 9.2 %all_to_all.44 = bf16[8,20,512]{2,1,0:T(8,128)(2,1)S(1)} all-to-all(bf16[8,20,512]{2,1,0:T(8,128)(2,1)S(1)} %broadcast_in_dim.20), channel_id=1, replica_groups=mesh['expert'=32,'vocab'=8] {'vocab'}, dimensions={0} | all-to-all | bytes 327680 | tf_op jit(solution)/shard_map/all_to_all | solution.py:12
  306.0 3.4 stack.3
  309.4 6.0 %all-to-all-start.5 = ((bf16[32,20,4096]{2,1,0:T(8,128)(2,1)}), bf16[32,20,4096]{2,1,0:T(8,128)(2,1)}, u32[]{:S(2)}, u32[]{:S(2)}) async-start(bf16[32,20,4096]{2,1,0:T(8,128)(2,1)} %stack.3), calls=%async_computation.6 | async-start | bytes 12582912 | tf_op jit(solution)/shard_map/all_to_all | solution.py:103
  315.5 140.7 %all-to-all-done.5 = bf16[32,20,4096]{2,1,0:T(8,128)(2,1)} async-done(((bf16[32,20,4096]{2,1,0:T(8,128)(2,1)}), bf16[32,20,4096]{2,1,0:T(8,128)(2,1)}, u32[]{:S(2)}, u32[]{:S(2)}) %all-to-all-start.5) | async-done | bytes 5242912 | tf_op jit(solution)/shard_map/all_to_all | solution.py:103
  456.1 7.8 %reshape.101 = bf16[640,4096]{1,0:T(8,128)(2,1)} reshape(bf16[32,20,4096]{2,1,0:T(8,128)(2,1)} %all-to-all-done.5) | data formatting | bytes 10485760 | tf_op jit(solution)/shard_map/reshape | solution.py:102
  464.0 6.3 %fusion.6 = f32[640,384]{1,0:T(8,128)} fusion(bf16[640,4096]{1,0:T(8,128)(2,1)} %reshape.101, bf16[384,4096]{1,0:T(8,128)(2,1)S(1)} %copy-done, pred[384]{0:T(512)(128)(4,1)S(1)} %broadcast_compare_fusion), kind=kOutput, calls=%fused_computation.15 | convolution fusion | flops 2013757440 | bytes 9372032 | tf_op jit(solution)/shard_map/dot_general | solution.py:101
  (52 shorter events, 4.8 us)
Async XLA Ops:
  7.2 456.8 %copy-start = (bf16[384,4096]{1,0:T(8,128)(2,1)S(1)}, bf16[384,4096]{1,0:T(8,128)(2,1)}, u32[]{:S(2)}) copy-start(bf16[384,4096]{1,0:T(8,128)(2,1)} %param.23) | copy-start | bytes 9437188
  7.2 127.4 %all-gather.2.cloned.1.call-start = ((), (), s32[]{:S(2)}) async-start(), calls=%async_computation.7 | async-start | bytes 11206656 | tf_op jit(solution)/shard_map/all_gather | solution.py:65
  80.4 146.6 %reduce-scatter.2.cloned.1.call-start = ((), (), s32[]{:S(2)}) async-start(), calls=%async_computation.8 | async-start | bytes 11206656 | tf_op jit(solution)/shard_map/reduce_scatter | solution.py:83
  134.6 8.6 %copy-start.2 = (bf16[1,1216,192]{1,2,0:T(8,128)(2,1)S(1)}, bf16[1,1216,192]{1,2,0:T(8,128)(2,1)}, u32[]{:S(2)}) copy-start(bf16[1,1216,192]{1,2,0:T(8,128)(2,1)} %param.18) | copy-start | bytes 1400836
  134.6 8.6 %copy-start.3 = (bf16[1,4096,192]{1,2,0:T(8,128)(2,1)S(1)}, bf16[1,4096,192]{1,2,0:T(8,128)(2,1)}, u32[]{:S(2)}) copy-start(bf16[1,4096,192]{1,2,0:T(8,128)(2,1)} %param.20) | copy-start | bytes 4718596
  134.6 8.6 %copy-start.5 = (bf16[1,1216,192]{1,2,0:T(8,128)(2,1)S(1)}, bf16[1,1216,192]{1,2,0:T(8,128)(2,1)}, u32[]{:S(2)}) copy-start(bf16[1,1216,192]{1,2,0:T(8,128)(2,1)} %param.19) | copy-start | bytes 1400836
  142.2 0.9 copy-start.1
  165.7 0.9 copy-start.4
  167.3 62.0 %all-to-all-start = ((f32[8,1,128]{2,1,0:T(1,128)}), f32[8,1,128]{2,1,0:T(1,128)S(1)}, u32[]{:S(2)}, u32[]{:S(2)}) async-start(f32[8,1,128]{2,1,0:T(1,128)} %broadcast_in_dim.16), calls=%async_computation | async-start | bytes 8192 | tf_op jit(solution)/shard_map/all_to_all | solution.py:12
  229.3 44.7 %all-to-all-start.2 = ((bf16[32,38,512]{2,1,0:T(8,128)(2,1)}), bf16[32,38,512]{2,1,0:T(8,128)(2,1)}, u32[]{:S(2)}, u32[]{:S(2)}) async-start(bf16[32,38,512]{2,1,0:T(8,128)(2,1)} %all_to_all.32), calls=%async_computation.3 | async-start | bytes 2621440 | tf_op jit(solution)/shard_map/all_to_all | solution.py:86
  283.6 2.1 copy-start.7
  286.5 8.9 %all-to-all-start.3 = ((f32[8,1,128]{2,1,0:T(1,128)}), f32[8,1,128]{2,1,0:T(1,128)S(1)}, u32[]{:S(2)}, u32[]{:S(2)}) async-start(f32[8,1,128]{2,1,0:T(1,128)} %broadcast_in_dim.18), calls=%async_computation.4 | async-start | bytes 8192 | tf_op jit(solution)/shard_map/all_to_all | solution.py:12
  296.5 9.4 %copy-start.6 = (bf16[128,512]{1,0:T(8,128)(2,1)}, bf16[128,512]{1,0:T(8,128)(2,1)S(1)}, u32[]{:S(2)}) copy-start(bf16[128,512]{1,0:T(8,128)(2,1)S(1)} %fusion.34) | copy-start | bytes 393220
  309.4 6.1 %copy-start.8 = (s32[384]{0:T(512)S(1)}, s32[384]{0:T(512)}, u32[]{:S(2)}) copy-start(s32[384]{0:T(512)} %param.24) | copy-start | bytes 4612
  309.4 146.7 %all-to-all-start.5 = ((bf16[32,20,4096]{2,1,0:T(8,128)(2,1)}), bf16[32,20,4096]{2,1,0:T(8,128)(2,1)}, u32[]{:S(2)}, u32[]{:S(2)}) async-start(bf16[32,20,4096]{2,1,0:T(8,128)(2,1)} %stack.3), calls=%async_computation.6 | async-start | bytes 12582912 | tf_op jit(solution)/shard_map/all_to_all | solution.py:103
Sparse Core Ops, SparseCore 0:
  80.5 54.0 all-gather.1
  165.9 61.0 reduce-scatter.1
